TPU v7x, 256 devices: a whole 4x4x8 slice. The times are simulated.
256 devices in a mesh: tile: 128 (over y, z, x), basin: 2 (over core).
Axes of the slice: x: 4, y: 4, z: 8, core: 2. Of those that a mesh axis runs over, the one named last changes fastest.
Arguments:
- cell_features: bfloat16 [65536, 512], P(('tile', 'basin')), may hold values from -6 to 6
- encoded: bfloat16 [1024, 512], P('tile'), may hold values from -6 to 6
- w_query: bfloat16 [512, 512], replicated, may hold values from -0.375 to 0.375
- w_key: bfloat16 [512, 512], replicated, may hold values from -0.375 to 0.375
- w_value: bfloat16 [512, 512], replicated, may hold values from -0.25 to 0.25
- w_out: bfloat16 [512, 512], replicated, may hold values from -0.25 to 0.25
- pattern: int32 [256, 16], P(('tile', 'basin')), may hold values from 0 to 127, all different within a row
- cell_basin: int32 [65536], P(('tile', 'basin')), may hold values from 0 to 511, as said below
- pooled_grad: bfloat16 [512, 512], P(('tile', 'basin')), may hold values from -24 to 24
Outputs:
- pooled: bfloat16 [512, 512], P(('tile', 'basin'))
- grad_cells: bfloat16 [65536, 512], P(('tile', 'basin'))
- grad_gauges: bfloat16 [1024, 512], P('tile')
- grad_query_weight: float32 [512, 512], replicated
- grad_key_weight: float32 [512, 512], replicated
- grad_value_weight: float32 [512, 512], replicated
- grad_out_weight: float32 [512, 512], replicated
Inputs may be any that keep to these rules, and one draw needn't show every extreme that they name: `pattern`: each row names 16 different gauge blocks; every block is named by some row. `cell_basin`: cell c lies in basin (2 * (c // 256) + k) mod 512 for some k with -2 <= k < 4; when c % 256 < 6, k = c % 256 - 2.
All inputs are finite; a program needn't handle non-finite values.
Results may differ from a plain program's by a relative error of at most 0.012.
The roundings to bfloat16 on the way count: a program that leaves them out, or rounds other values in their place, can miss the bound.
Values may be sent and summed in bfloat16 or wider, within the bound.
No kernel may reach another device: no remote copies, remote signals or barrier semaphores. Data moves between devices by JAX's collectives and lax.ppermute only.
A program may use at most 64 MiB of HBM per device.

v0:
```python
import math
import jax
import jax.numpy as jnp
from jax import lax
from jax.sharding import PartitionSpec as P

HEADS = 8
HEAD_DIM = 64
score_cap = 30.0


def shifted(value, axis, steps):
    count = lax.axis_size(axis)
    pairs = [(source, (source + steps) % count) for source in range(count)]
    return lax.ppermute(value, axis, pairs)


def forward_heads(queries, key_sel, value_sel):
    row_count = queries.shape[0]
    key_count = key_sel.shape[0]
    query_heads = queries.reshape(row_count, HEADS, HEAD_DIM)
    key_heads = key_sel.reshape(key_count, HEADS, HEAD_DIM)
    value_heads = value_sel.reshape(key_count, HEADS, HEAD_DIM)
    scores = jnp.einsum(
        "rhd,khd->hrk", query_heads, key_heads, preferred_element_type=jnp.float32
    ) * (1.0 / math.sqrt(HEAD_DIM))
    tanh_val = jnp.tanh(scores / score_cap)
    exponent = jnp.exp(score_cap * tanh_val)
    weights = exponent / jnp.sum(exponent, axis=-1, keepdims=True)
    weights_bf = weights.astype(jnp.bfloat16)
    attended = jnp.einsum(
        "hrk,khd->rhd", weights_bf, value_heads, preferred_element_type=jnp.float32
    )
    attended = attended.reshape(row_count, HEADS * HEAD_DIM).astype(jnp.bfloat16)
    return (attended, weights, weights_bf, tanh_val)


def backward_heads(queries, key_sel, value_sel, weights, weights_bf, tanh_val, attended_grad):
    row_count = queries.shape[0]
    key_count = key_sel.shape[0]
    query_heads = queries.reshape(row_count, HEADS, HEAD_DIM)
    key_heads = key_sel.reshape(key_count, HEADS, HEAD_DIM)
    value_heads = value_sel.reshape(key_count, HEADS, HEAD_DIM)
    grad_heads = attended_grad.reshape(row_count, HEADS, HEAD_DIM)
    weight_grad = jnp.einsum(
        "rhd,khd->hrk", grad_heads, value_heads, preferred_element_type=jnp.float32
    )
    value_grad = jnp.einsum(
        "hrk,rhd->khd", weights_bf, grad_heads, preferred_element_type=jnp.float32
    )
    inner_sum = jnp.sum(weights * weight_grad, axis=-1, keepdims=True)
    score_grad = (
        weights
        * (weight_grad - inner_sum)
        * (1.0 - tanh_val * tanh_val)
        * (1.0 / math.sqrt(HEAD_DIM))
    )
    score_grad = score_grad.astype(jnp.bfloat16)
    query_grad = jnp.einsum(
        "hrk,khd->rhd", score_grad, key_heads, preferred_element_type=jnp.float32
    )
    query_grad = query_grad.reshape(row_count, HEADS * HEAD_DIM).astype(jnp.bfloat16)
    key_grad = jnp.einsum(
        "hrk,rhd->khd", score_grad, query_heads, preferred_element_type=jnp.float32
    )
    return (
        query_grad,
        key_grad.reshape(key_count, HEADS * HEAD_DIM),
        value_grad.reshape(key_count, HEADS * HEAD_DIM),
    )


def fetch_gauges(moving):
    return lax.all_gather(moving, "tile", axis=0, tiled=True)


def sum_cores(partial_value):
    return lax.psum(partial_value, "basin")


def contract_rows(left_side, right_side):
    return lax.dot_general(
        left_side, right_side, (((0,), (0,)), ((), ())), preferred_element_type=jnp.float32
    )


def contract_cols(left_side, right_side):
    return lax.dot_general(
        left_side, right_side, (((1,), (1,)), ((), ())), preferred_element_type=jnp.float32
    )


def per_device(
    cell_features, encoded, w_query, w_key, w_value, w_out, pattern, cell_basin, pooled_grad
):
    highest = lax.Precision.HIGHEST
    cell_count = cell_features.shape[0]
    model_width = cell_features.shape[1]
    gauge_rows = encoded.shape[0]
    chosen_blocks = pattern[0]
    block_count = chosen_blocks.shape[0]
    tile_count = lax.axis_size("tile")
    queries = jnp.dot(cell_features, w_query, preferred_element_type=jnp.float32).astype(
        jnp.bfloat16
    )
    own_keys = jnp.dot(encoded, w_key, preferred_element_type=jnp.float32).astype(jnp.bfloat16)
    own_values = jnp.dot(encoded, w_value, preferred_element_type=jnp.float32).astype(jnp.bfloat16)
    moving = jnp.concatenate([own_keys, own_values], axis=1)
    gathered = fetch_gauges(moving)
    shaped = gathered.reshape(tile_count, gauge_rows, gathered.shape[1])
    picked = jnp.take(shaped, chosen_blocks, axis=0).reshape(
        block_count * gauge_rows, gathered.shape[1]
    )
    key_sel = picked[:, :model_width]
    value_sel = picked[:, model_width:]
    block_rows = min(512, cell_count)
    block_total = cell_count // block_rows
    query_blocks = queries.reshape(block_total, block_rows, model_width)

    def attend_block(query_block):
        return forward_heads(query_block, key_sel, value_sel)[0]

    attended = lax.map(attend_block, query_blocks).reshape(cell_count, model_width)
    cell_out = jnp.dot(attended, w_out, preferred_element_type=jnp.float32).astype(jnp.bfloat16)
    device = lax.axis_index(("tile", "basin"))
    own_basins = pooled_grad.shape[0]
    basin_total = own_basins * lax.axis_size(("tile", "basin"))
    basin_slot = (cell_basin - device * own_basins + own_basins) % basin_total
    slot_count = 3 * own_basins
    onehot = (basin_slot[:, None] == jnp.arange(slot_count, dtype=jnp.int32)[None, :]).astype(
        jnp.bfloat16
    )
    basin_sums = contract_rows(onehot, cell_out)
    slot_counts = jnp.sum(onehot, axis=0, dtype=jnp.float32)
    lower_part = (basin_sums[:own_basins], slot_counts[:own_basins])
    upper_part = (basin_sums[2 * own_basins :], slot_counts[2 * own_basins :])
    from_above = shifted((lower_part[0], lower_part[1]), ("tile", "basin"), -1)
    from_below = shifted((upper_part[0], upper_part[1]), ("tile", "basin"), 1)
    own_sums = basin_sums[own_basins : 2 * own_basins] + from_above[0] + from_below[0]
    own_counts = slot_counts[own_basins : 2 * own_basins] + from_above[1] + from_below[1]
    count_root = jnp.sqrt(own_counts)
    pooled = (own_sums / count_root[:, None]).astype(jnp.bfloat16)
    scaled_table = pooled_grad.astype(jnp.float32) / count_root[:, None]
    below_table = shifted(scaled_table, ("tile", "basin"), 1)
    above_table = shifted(scaled_table, ("tile", "basin"), -1)
    grad_table = jnp.concatenate([below_table, scaled_table, above_table], axis=0)
    out_grad = jnp.take(grad_table, basin_slot, axis=0).astype(jnp.bfloat16)
    grad_out_local = contract_rows(attended, out_grad)
    attended_grad = contract_cols(out_grad, w_out).astype(jnp.bfloat16)
    grad_blocks = attended_grad.reshape(block_total, block_rows, model_width)

    def backward_block(running, pieces):
        query_block, grad_block = pieces
        unused, weights, weights_bf, tanh_val = forward_heads(query_block, key_sel, value_sel)
        query_grad, key_grad, value_grad = backward_heads(
            query_block, key_sel, value_sel, weights, weights_bf, tanh_val, grad_block
        )
        return ((running[0] + key_grad, running[1] + value_grad), query_grad)

    empty = jnp.zeros((key_sel.shape[0], model_width), jnp.float32)
    (key_grad_sel, value_grad_sel), query_grad = lax.scan(
        backward_block, (empty, empty), (query_blocks, grad_blocks)
    )
    query_grad = query_grad.reshape(cell_count, model_width)
    grad_query_local = contract_rows(cell_features, query_grad)
    grad_cells = contract_cols(query_grad, w_query).astype(jnp.bfloat16)
    both_grads = jnp.concatenate([key_grad_sel, value_grad_sel], axis=1)
    both_weights = jnp.concatenate([w_key, w_value], axis=1).astype(jnp.float32)
    column_width = both_grads.shape[1]
    return_term = jnp.zeros((tile_count, gauge_rows, column_width), jnp.float32)
    return_term = return_term.at[chosen_blocks].set(
        both_grads.reshape(block_count, gauge_rows, column_width)
    )
    return_term = return_term.reshape(tile_count * gauge_rows, column_width)
    returned = lax.psum_scatter(return_term, "tile", scatter_dimension=0, tiled=True)
    pair_local = lax.dot_general(
        encoded.astype(jnp.float32), returned, (((0,), (0,)), ((), ())), precision=highest
    )
    partial_value = lax.dot_general(
        returned, both_weights, (((1,), (1,)), ((), ())), precision=highest
    )
    grad_gauges = sum_cores(partial_value)
    grad_gauges = grad_gauges.astype(jnp.bfloat16)
    summed = lax.psum((grad_query_local, grad_out_local, pair_local), ("tile", "basin"))
    grad_query_weight = summed[0]
    grad_out_weight = summed[1]
    grad_key_weight = summed[2][:, :model_width]
    grad_value_weight = summed[2][:, model_width:]
    return (
        pooled,
        grad_cells,
        grad_gauges,
        grad_query_weight,
        grad_key_weight,
        grad_value_weight,
        grad_out_weight,
    )


def solution(mesh):
    return jax.shard_map(
        per_device,
        mesh=mesh,
        in_specs=(
            P(("tile", "basin"), None),
            P("tile", None),
            P(),
            P(),
            P(),
            P(),
            P(("tile", "basin"), None),
            P(("tile", "basin")),
            P(("tile", "basin"), None),
        ),
        out_specs=(
            P(("tile", "basin"), None),
            P(("tile", "basin"), None),
            P("tile", None),
            P(),
            P(),
            P(),
            P(),
        ),
        check_vma=False,
    )
```

profile of v0, /device:TPU:8, one launch (start us, length us, event | category | flops | bytes accessed | tf_op | source)
XLA Modules:
  0.0 1125.6 jit_solution(10916404886895113197)
XLA Ops:
  7.2 1.3 convolution_convert_fusion.6
  8.5 1.2 convolution_convert_fusion.7
  11.4 7.5 collective-permute-start.2
  20.2 1.2 convolution_convert_fusion.5
  21.6 4.6 collective-permute-start.5
  27.5 5.9 collective-permute-done.4
  33.4 1.2 gather_fusion.1
  35.1 94.1 %all-gather.2.cloned.1.call-done = bf16[1024,1024]{1,0:T(8,128)(2,1)} async-done(((bf16[8,1024]{1,0:T(8,128)(2,1)}), bf16[1024,1024]{1,0:T(8,128)(2,1)}) %all-gather.2.cloned.1.call-update) | async-done | bytes 2097168 | tf_op jit(solution)/shard_map/all_gather | solution.py:74
  129.1 2.2 gather_fusion
  133.8 2.3 convolution_bitcast_fusion.3
  136.5 2.5 broadcast_in_dim.53
  139.0 2.6 scatter_fusion
  141.6 1.1 copy-done.11
  144.4 1.3 convolution_bitcast_fusion.1
  145.7 1.3 fusion.39
  147.0 617.3 %reduce-scatter.2.cloned.1.call-done = f32[8,1024]{1,0:T(8,128)} async-done(((f32[1024,1024]{1,0:T(8,128)}), f32[8,1024]{1,0:T(8,128)}) %reduce-scatter.2.cloned.1.call-update) | async-done | bytes 32784 | tf_op jit(solution)/shard_map/reduce_scatter | solution.py:175
  764.4 3.1 convolution_bitcast_fusion
  769.0 6.0 collective-permute-start
  777.8 4.0 psum.28
  781.8 329.4 %all-reduce.3.cloned.1.call-done = (f32[512,512]{0,1:T(8,128)}, f32[512,1024]{0,1:T(8,128)}, f32[512,512]{1,0:T(8,128)}) async-done(((f32[512,512]{0,1:T(8,128)}, f32[512,1024]{0,1:T(8,128)}, f32[512,512]{1,0:T(8,128)}), (f32[512,512]{0,1:T(8,128)}, f32[512,1024]{0,1:T(8,128)}, f32[512,512]{1,0:T(8,128)})) %all-reduce.3.cloned.1.call-update) | async-done | bytes 4194320 | tf_op jit(solution)/shard_map/psum | solution.py:184
  1111.2 2.5 copy.49
  1113.7 1.7 fusion.46
  1115.5 1.3 copy.50
  1116.8 1.3 copy.51
  (73 shorter events, 14.7 us)
Async XLA Ops:
  7.2 13.0 %copy-start = (bf16[512,512]{1,0:T(8,128)(2,1)S(1)}, bf16[512,512]{1,0:T(8,128)(2,1)}, u32[]{:S(2)}) copy-start(bf16[512,512]{1,0:T(8,128)(2,1)} %param.11) | copy-start | bytes 1572868
  7.2 14.3 %copy-start.7 = (bf16[2,512]{1,0:T(2,128)(2,1)S(1)}, bf16[2,512]{1,0:T(2,128)(2,1)}, u32[]{:S(2)}) copy-start(bf16[2,512]{1,0:T(2,128)(2,1)} %param.17) | copy-start | bytes 6148
  7.2 122.0 %all-gather.2.cloned.1.call-start = ((), (), s32[]{:S(2)}) async-start(), calls=%async_computation.1 | async-start | bytes 2113536 | tf_op jit(solution)/shard_map/all_gather | solution.py:74
  9.8 24.8 %copy-start.8 = (bf16[512,512]{1,0:T(8,128)(2,1)S(1)}, bf16[512,512]{1,0:T(8,128)(2,1)}, u32[]{:S(2)}) copy-start(bf16[512,512]{1,0:T(8,128)(2,1)} %param.14) | copy-start | bytes 1572868
  10.4 754.0 %reduce-scatter.2.cloned.1.call-start = ((), (), s32[]{:S(2)}) async-start(), calls=%async_computation.2 | async-start | bytes 4227072 | tf_op jit(solution)/shard_map/reduce_scatter | solution.py:175
  11.3 10.1 collective-permute-start.3
  11.4 10.1 collective-permute-start.2
  21.6 5.9 collective-permute-start.5
  26.2 7.2 collective-permute-start.4
  132.1 1.0 copy-start.10
  141.5 1.2 copy-start.11
  141.6 969.7 %all-reduce.3.cloned.1.call-start = ((), (), s32[]{:S(2)}) async-start(), calls=%async_computation.3 | async-start | bytes 8388608 | tf_op jit(solution)/shard_map/psum | solution.py:184
  143.5 1.0 copy-start.2
  143.8 620.6 %copy-start.5 = (bf16[8,512]{1,0:T(8,128)(2,1)S(1)}, bf16[8,512]{1,0:T(8,128)(2,1)}, u32[]{:S(2)}) copy-start(bf16[8,512]{1,0:T(8,128)(2,1)} %param.10) | copy-start | bytes 24580
  767.5 1.0 copy-start.9
  767.5 9.4 copy-start.3
  767.5 9.4 copy-start.4
  767.5 9.4 copy-start.6
  769.0 7.3 collective-permute-start.1
  769.0 7.3 collective-permute-start
  1116.8 1.3 copy-start.1
Sparse Core Ops, SparseCore 0:
  12.2 116.8 all-gather.1
  141.7 622.6 reduce-scatter.1
  771.8 339.3 all-reduce.2
where the time goes:
time: 1130 us
  waiting for transfers between devices  1050 us (93%)
  local copies, waits for them, and re-layouts  21.1 us (2%)
  starting transfers between devices  18.1 us (2%)
  matrix products  16.7 us (1%)
  between operations  14 us (1%)
    reduce_scatter x1, waiting for transfers between devices, per_device(): lax.psum_scatter(return_term, 'tile', scatter_dimension=0, tiled=True)  617 us
    psum x1, waiting for transfers between devices, per_device(): lax.psum((grad_query_local, grad_out_local, pair_local), ('tile', 'basin'))  329 us
    all_gather x1, waiting for transfers between devices, fetch_gauges(): return lax.all_gather(moving, 'tile', axis=0, tiled=True)  94.1 us
  transfers between devices with their start and end apart: 9, of which 6 were waited for; matrix products, arithmetic and copies ran while one was open for 1% of the time, Pallas kernels for 0%

commit v1 on v0

--- a/solution.py
+++ b/solution.py
@@ -7,6 +7,11 @@
 HEADS = 8
 HEAD_DIM = 64
 score_cap = 30.0
+
+
+def all_by_exchange(value, axis, along):
+    outgoing = jnp.stack([value] * lax.axis_size(axis))
+    return jnp.concatenate(lax.all_to_all(outgoing, axis, 0, 0), axis=along)
 
 
 def shifted(value, axis, steps):
@@ -71,7 +76,7 @@
 
 
 def fetch_gauges(moving):
-    return lax.all_gather(moving, "tile", axis=0, tiled=True)
+    return all_by_exchange(moving, "tile", 0)
 
 
 def sum_cores(partial_value):

time: 1130 us -> 1080 us (0.956)
  waiting for transfers between devices: 1050 us -> 992 us
  starting transfers between devices: 18.1 us -> 31.2 us
    all_gather x1 -> x0, waiting for transfers between devices: 94.1 us -> none  [fetch_gauges(): return lax.all_gather(moving, 'tile', axis=0, tiled=True)]
    ppermute x6, waiting for transfers between devices: 7.18 us -> 45 us  [shifted(): return lax.ppermute(value, axis, pairs)]
    all_to_all x0 -> x1, starting transfers between devices: none -> 15.6 us  [all_by_exchange(): return jnp.concatenate(lax.all_to_all(outgoing, axis, 0, 0), axis=along)]
where the time goes in v1:
time: 1080 us
  waiting for transfers between devices  992 us (92%)
  starting transfers between devices  31.2 us (3%)
  matrix products  20.6 us (2%)
  local copies, waits for them, and re-layouts  20.3 us (2%)
  between operations  14.3 us (1%)
    reduce_scatter x1, waiting for transfers between devices, per_device(): lax.psum_scatter(return_term, 'tile', scatter_dimension=0, tiled=True)  617 us
    psum x1, waiting for transfers between devices, per_device(): lax.psum((grad_query_local, grad_out_local, pair_local), ('tile', 'basin'))  329 us
    ppermute x6, waiting for transfers between devices, shifted(): return lax.ppermute(value, axis, pairs)  45 us
  transfers between devices with their start and end apart: 9, of which 6 were waited for; matrix products, arithmetic and copies ran while one was open for 1% of the time, Pallas kernels for 0%

profile of v1, /device:TPU:8, one launch (start us, length us, event | category | flops | bytes accessed | tf_op | source)
XLA Modules:
  0.0 1083.1 jit_solution(15357050202038501873)
XLA Ops:
  7.2 1.3 convolution_convert_fusion.6
  9.7 1.6 stack.2
  11.3 15.6 %all-to-all-start = ((bf16[128,8,1024]{2,1,0:T(8,128)(2,1)}), bf16[128,8,1024]{2,1,0:T(8,128)(2,1)S(1)}, u32[]{:S(2)}, u32[]{:S(2)}) async-start(bf16[128,8,1024]{2,1,0:T(8,128)(2,1)} %stack.2), calls=%async_computation | async-start | bytes 4194304 | tf_op jit(solution)/shard_map/all_to_all | solution.py:14
  27.2 6.0 collective-permute-start.2
  33.5 38.5 %collective-permute-done.3 = f32[2]{0:T(128)S(1)} collective-permute-done((f32[2]{0:T(128)S(1)}, f32[2]{0:T(128)S(1)}, u32[]{:S(2)}, u32[]{:S(2)}) %collective-permute-start.3) | collective-permute-done | bytes 40 | tf_op jit(solution)/shard_map/ppermute | solution.py:20
  72.2 3.4 collective-permute-start.5
  76.9 5.9 collective-permute-done.4
  84.0 1.4 convolution_convert_fusion.2
  86.5 1.5 fusion.18
  89.9 2.3 convolution_bitcast_fusion.3
  92.6 2.5 broadcast_in_dim.53
  95.1 2.6 scatter_fusion
  97.9 2.3 convolution_convert_fusion.1
  100.3 1.6 convolution_convert_fusion.4
  103.1 1.3 fusion.39
  104.5 617.0 %reduce-scatter.2.cloned.1.call-done = f32[8,1024]{1,0:T(8,128)} async-done(((f32[1024,1024]{1,0:T(8,128)}), f32[8,1024]{1,0:T(8,128)}) %reduce-scatter.2.cloned.1.call-update) | async-done | bytes 32784 | tf_op jit(solution)/shard_map/reduce_scatter | solution.py:180
  721.5 3.1 convolution_bitcast_fusion
  726.1 6.0 collective-permute-start
  735.0 4.0 psum.28
  738.9 329.5 %all-reduce.3.cloned.1.call-done = (f32[512,512]{0,1:T(8,128)}, f32[512,1024]{0,1:T(8,128)}, f32[512,512]{1,0:T(8,128)}) async-done(((f32[512,512]{0,1:T(8,128)}, f32[512,1024]{0,1:T(8,128)}, f32[512,512]{1,0:T(8,128)}), (f32[512,512]{0,1:T(8,128)}, f32[512,1024]{0,1:T(8,128)}, f32[512,512]{1,0:T(8,128)})) %all-reduce.3.cloned.1.call-update) | async-done | bytes 4194320 | tf_op jit(solution)/shard_map/psum | solution.py:189
  1068.4 2.5 copy.50
  1070.9 1.7 fusion.46
  1072.6 1.3 copy.51
  1074.0 1.3 copy.52
  (78 shorter events, 14.7 us)
Async XLA Ops:
  7.2 26.1 %copy-start = (bf16[512,512]{1,0:T(8,128)(2,1)S(1)}, bf16[512,512]{1,0:T(8,128)(2,1)}, u32[]{:S(2)}) copy-start(bf16[512,512]{1,0:T(8,128)(2,1)} %param.11) | copy-start | bytes 1572868
  11.3 15.7 %copy-start.10 = (s32[256]{0:T(256)S(1)}, s32[256]{0:T(256)}, u32[]{:S(2)}) copy-start(s32[256]{0:T(256)} %param.16) | copy-start | bytes 3076
  11.3 21.9 %copy-start.12 = (s32[1,16]{1,0:T(1,128)S(1)}, s32[1,16]{1,0:T(1,128)}, u32[]{:S(2)}) copy-start(s32[1,16]{1,0:T(1,128)} %param.15) | copy-start | bytes 196
  11.3 21.9 %copy-start.2 = (bf16[256,512]{1,0:T(8,128)(2,1)S(1)}, bf16[256,512]{1,0:T(8,128)(2,1)}, u32[]{:S(2)}) copy-start(bf16[256,512]{1,0:T(8,128)(2,1)} %param.9) | copy-start | bytes 786436
  11.3 60.8 %copy-start.9 = (bf16[2,512]{1,0:T(2,128)(2,1)S(1)}, bf16[2,512]{1,0:T(2,128)(2,1)}, u32[]{:S(2)}) copy-start(bf16[2,512]{1,0:T(2,128)(2,1)} %param.17) | copy-start | bytes 6148
  11.3 74.2 %all-to-all-start = ((bf16[128,8,1024]{2,1,0:T(8,128)(2,1)}), bf16[128,8,1024]{2,1,0:T(8,128)(2,1)S(1)}, u32[]{:S(2)}, u32[]{:S(2)}) async-start(bf16[128,8,1024]{2,1,0:T(8,128)(2,1)} %stack.2), calls=%async_computation | async-start | bytes 4194304 | tf_op jit(solution)/shard_map/all_to_all | solution.py:14
  26.9 694.6 %reduce-scatter.2.cloned.1.call-start = ((), (), s32[]{:S(2)}) async-start(), calls=%async_computation.2 | async-start | bytes 4227072 | tf_op jit(solution)/shard_map/reduce_scatter | solution.py:180
  27.2 44.8 %collective-permute-start.3 = (f32[2]{0:T(128)S(1)}, f32[2]{0:T(128)S(1)}, u32[]{:S(2)}, u32[]{:S(2)}) collective-permute-start(f32[2]{0:T(128)S(1)} %get-tuple-element.79), channel_id=1, source_target_pairs={{0,1},{1,2},{2,3},{3,4},{4,5},{5,6},{6,7},{7,8},{8,9},{9,10},{10,1... | collective-permute-start | bytes 32 | tf_op jit(solution)/shard_map/ppermute | solution.py:20
  27.2 44.8 %collective-permute-start.2 = (f32[2]{0:T(128)S(1)}, f32[2]{0:T(128)S(1)}, u32[]{:S(2)}, u32[]{:S(2)}) collective-permute-start(f32[2]{0:T(128)S(1)} %get-tuple-element.78), channel_id=1, source_target_pairs={{0,255},{1,0},{2,1},{3,2},{4,3},{5,4},{6,5},{7,6},{8,7},{9,8},{10,... | collective-permute-start | bytes 32 | tf_op jit(solution)/shard_map/ppermute | solution.py:20
  72.2 4.7 collective-permute-start.5
  75.6 7.2 collective-permute-start.4
  88.0 1.0 copy-start.13
  89.0 0.9 copy-start.6
  97.7 970.7 %all-reduce.3.cloned.1.call-start = ((), (), s32[]{:S(2)}) async-start(), calls=%async_computation.3 | async-start | bytes 8388608 | tf_op jit(solution)/shard_map/psum | solution.py:189
  100.2 1.6 copy-start.3
  101.9 619.7 %copy-start.7 = (bf16[8,512]{1,0:T(8,128)(2,1)S(1)}, bf16[8,512]{1,0:T(8,128)(2,1)}, u32[]{:S(2)}) copy-start(bf16[8,512]{1,0:T(8,128)(2,1)} %param.10) | copy-start | bytes 24580
  724.6 1.0 copy-start.11
  724.6 9.4 copy-start.4
  724.6 9.4 copy-start.5
  724.6 9.4 copy-start.8
  726.1 7.3 collective-permute-start.1
  726.1 7.3 collective-permute-start
  1073.9 1.3 copy-start.1
Sparse Core Ops, SparseCore 0:
  97.8 623.6 reduce-scatter.1
  728.9 339.4 all-reduce.2
